TPU v7x, 32 devices: a whole 2x2x4 slice. The times are simulated.
32 devices in a mesh: rep: 2 (over x), shard: 4 (over y, core), ctx: 4 (over z).
Axes of the slice: x: 2, y: 2, z: 4, core: 2. Of those that a mesh axis runs over, the one named last changes fastest.
Arguments:
- tokens: bfloat16 [16, 256, 1024], P(('rep', 'shard'), 'ctx'), may hold values from -6 to 6
- positions: int32 [16, 256], P(('rep', 'shard')), may hold values from 0 to 255, as said below
- segments: int32 [16, 256], P(('rep', 'shard')), may hold values from 0 to 2, as said below
- cotangent: bfloat16 [16, 256, 1024], P(('rep', 'shard'), 'ctx'), may hold values from -6 to 6
- w_query: bfloat16 [1024, 2048], P(None, ('shard', 'ctx')), may hold values from -0.1875 to 0.1875
- key_weight: bfloat16 [1024, 1024], P(None, ('shard', 'ctx')), may hold values from -0.1875 to 0.1875
- value_weight: bfloat16 [1024, 1024], P(None, ('shard', 'ctx')), may hold values from -0.1875 to 0.1875
- output_weight: bfloat16 [2048, 1024], P(('shard', 'ctx')), may hold values from -0.625 to 0.625
- w_gate: bfloat16 [1024, 3072], P(None, ('shard', 'ctx')), may hold values from -0.1875 to 0.1875
- w_up: bfloat16 [1024, 3072], P(None, ('shard', 'ctx')), may hold values from -0.1875 to 0.1875
- w_down: bfloat16 [3072, 1024], P(('shard', 'ctx')), may hold values from -0.109375 to 0.109375
- norm_gains: bfloat16 [2304], P(('shard', 'ctx')), may hold values from 0.5 to 1.5
Outputs:
- block_out: bfloat16 [16, 256, 1024], P(('rep', 'shard'), 'ctx')
- grad_input: float32 [16, 256, 1024], P(('rep', 'shard'), 'ctx')
- grad_query: float32 [1024, 2048], P(None, ('shard', 'ctx'))
- grad_key: float32 [1024, 1024], P(None, ('shard', 'ctx'))
- grad_value: float32 [1024, 1024], P(None, ('shard', 'ctx'))
- grad_output: float32 [2048, 1024], P(('shard', 'ctx'))
- grad_gate: float32 [1024, 3072], P(None, ('shard', 'ctx'))
- grad_up: float32 [1024, 3072], P(None, ('shard', 'ctx'))
- grad_down: float32 [3072, 1024], P(('shard', 'ctx'))
- grad_gains: float32 [2304], P(('shard', 'ctx'))
Inputs may be any that keep to these rules, and one draw needn't show every extreme that they name: In each sequence the stored positions are a permutation of all its positions made of runs of 32 consecutive positions; the two runs held by one index of ctx are the k-th from the start and the k-th from the end of the sequence, with k drawn per sequence. `segments`: ordered by position, a sequence's document numbers never fall, start at 0 and use every number up to 2.
All inputs are finite; a program needn't handle non-finite values.
Results may differ from a plain program's by a relative error of at most 0.02.
Values may be sent and summed in bfloat16 or wider, within the bound.
A program may use at most 192 MiB of HBM per device.

v0:
```python
import math

import jax
import jax.numpy as jnp
from jax import lax
from jax.sharding import PartitionSpec as P

QUERY_HEADS = 16
KEY_VALUE_HEADS = 8
HEAD_DIM = 128


EPSILON = 1e-06
ROPE_BASE = 1000000.0


def rms_scale(values_in):
    return lax.rsqrt(jnp.mean(values_in * values_in, axis=-1, keepdims=True) + EPSILON)


def norm_backward(grad_in, values_in, scale_in, gain_in):
    grad_norm = grad_in * gain_in
    unit = values_in * scale_in
    return scale_in * (grad_norm - unit * jnp.mean(grad_norm * unit, axis=-1, keepdims=True))


def rope_tables(position_ids):
    half_dim = HEAD_DIM // 2
    inverse = 1.0 / ROPE_BASE ** (jnp.arange(half_dim, dtype=jnp.float32) * (2.0 / HEAD_DIM))
    angle = position_ids.astype(jnp.float32)[..., None] * inverse
    return (jnp.cos(angle)[:, :, None, :], jnp.sin(angle)[:, :, None, :])


def rotate(values_in, cosine, sine):
    half_dim = values_in.shape[-1] // 2
    first = values_in[..., :half_dim]
    second = values_in[..., half_dim:]
    return jnp.concatenate(
        [first * cosine - second * sine, second * cosine + first * sine], axis=-1
    )


def rotate_back(grad_in, cosine, sine):
    half_dim = grad_in.shape[-1] // 2
    first = grad_in[..., :half_dim]
    second = grad_in[..., half_dim:]
    return jnp.concatenate(
        [first * cosine + second * sine, second * cosine - first * sine], axis=-1
    )


def float_product(left, right):
    return jnp.dot(left, right, preferred_element_type=jnp.float32)


def against_rows(left, right):
    return lax.dot_general(
        left, right, (((1,), (1,)), ((), ())), preferred_element_type=jnp.float32
    )


def over_tokens(left, right):
    return lax.dot_general(
        left, right, (((0,), (0,)), ((), ())), preferred_element_type=jnp.float32
    )


def body(
    tokens,
    positions,
    segments,
    cotangent,
    w_query,
    key_weight,
    value_weight,
    output_weight,
    w_gate,
    w_up,
    w_down,
    norm_gains,
):
    sequence_count, local_length, model_width = tokens.shape
    total_rows = sequence_count * local_length
    group_width = QUERY_HEADS // KEY_VALUE_HEADS
    score_scale = 1.0 / math.sqrt(HEAD_DIM)
    local_start = lax.axis_index("ctx") * local_length
    local_pos = lax.dynamic_slice_in_dim(positions, local_start, local_length, 1)
    local_seg = lax.dynamic_slice_in_dim(segments, local_start, local_length, 1)
    wq_full, full_key_weight, full_value_weight, wo_full, gains_full = (
        lax.all_gather(w_query, ("shard", "ctx"), axis=1, tiled=True),
        lax.all_gather(key_weight, ("shard", "ctx"), axis=1, tiled=True),
        lax.all_gather(value_weight, ("shard", "ctx"), axis=1, tiled=True),
        lax.all_gather(output_weight, ("shard", "ctx"), axis=0, tiled=True),
        lax.all_gather(norm_gains, ("shard", "ctx"), axis=0, tiled=True),
    )
    gain_all = gains_full.astype(jnp.float32)
    g_attn = gain_all[:model_width]
    g_query = gain_all[model_width : model_width + HEAD_DIM]
    key_gain = gain_all[model_width + HEAD_DIM : model_width + 2 * HEAD_DIM]
    g_mlp = gain_all[model_width + 2 * HEAD_DIM :]
    x_rows = tokens.reshape(total_rows, model_width).astype(jnp.float32)
    scale_in = rms_scale(x_rows)
    normed_input = (x_rows * scale_in * g_attn).astype(jnp.bfloat16)
    query = float_product(normed_input, wq_full).reshape(
        sequence_count, local_length, QUERY_HEADS, HEAD_DIM
    )
    key_rows = float_product(normed_input, full_key_weight).reshape(
        sequence_count, local_length, KEY_VALUE_HEADS, HEAD_DIM
    )
    value_rows = (
        float_product(normed_input, full_value_weight)
        .astype(jnp.bfloat16)
        .reshape(sequence_count, local_length, KEY_VALUE_HEADS, HEAD_DIM)
    )
    q_scale = rms_scale(query)
    key_scale = rms_scale(key_rows)
    cosine, sine = rope_tables(local_pos)
    query_rotated = rotate(query * q_scale * g_query, cosine, sine).astype(jnp.bfloat16)
    k_rot = rotate(key_rows * key_scale * key_gain, cosine, sine).astype(jnp.bfloat16)
    keys_all, values_all = (
        lax.all_gather(k_rot, "ctx", axis=1, tiled=True),
        lax.all_gather(value_rows, "ctx", axis=1, tiled=True),
    )
    allowed = (
        (local_seg[:, :, None] == segments[:, None, :])
        & (positions[:, None, :] <= local_pos[:, :, None])
    )[:, None, None]
    query_group = query_rotated.reshape(
        sequence_count, local_length, KEY_VALUE_HEADS, group_width, HEAD_DIM
    )
    scores = (
        jnp.einsum("bqkgd,bskd->bkgqs", query_group, keys_all, preferred_element_type=jnp.float32)
        * score_scale
    )
    exponent = jnp.where(allowed, jnp.exp(scores), 0.0)
    denominator = jnp.sum(exponent, axis=-1)
    log_total = jnp.log(denominator)
    probs = (exponent / denominator[..., None]).astype(jnp.bfloat16)
    attention_output = jnp.einsum(
        "bkgqs,bskd->bqkgd", probs, values_all, preferred_element_type=jnp.float32
    )
    attention_output = attention_output.astype(jnp.bfloat16).reshape(
        total_rows, QUERY_HEADS * HEAD_DIM
    )
    mixed_in = x_rows + float_product(attention_output, wo_full)
    scale_mid = rms_scale(mixed_in)
    normed_mid = (mixed_in * scale_mid * g_mlp).astype(jnp.bfloat16)
    wg_full, wu_full, wd_full = (
        lax.all_gather(w_gate, ("shard", "ctx"), axis=1, tiled=True),
        lax.all_gather(w_up, ("shard", "ctx"), axis=1, tiled=True),
        lax.all_gather(w_down, ("shard", "ctx"), axis=0, tiled=True),
    )
    gate_pre = float_product(normed_mid, wg_full)
    up_pre = float_product(normed_mid, wu_full)
    sigmoid_gate = jax.nn.sigmoid(gate_pre)
    hidden = (gate_pre * sigmoid_gate * up_pre).astype(jnp.bfloat16)
    block_sum = mixed_in + float_product(hidden, wd_full)
    block_out = block_sum.astype(jnp.bfloat16).reshape(sequence_count, local_length, model_width)
    grad_rows = cotangent.reshape(total_rows, model_width)
    d_hidden = against_rows(grad_rows, wd_full)
    grad_down = over_tokens(hidden, grad_rows)
    d_gate = (d_hidden * up_pre * sigmoid_gate * (1.0 + gate_pre * (1.0 - sigmoid_gate))).astype(
        jnp.bfloat16
    )
    d_up = (d_hidden * gate_pre * sigmoid_gate).astype(jnp.bfloat16)
    grad_gate = over_tokens(normed_mid, d_gate)
    grad_up = over_tokens(normed_mid, d_up)
    owned_gate, owned_up, owned_down = (
        lax.psum_scatter(grad_gate, ("shard", "ctx"), scatter_dimension=1, tiled=True),
        lax.psum_scatter(grad_up, ("shard", "ctx"), scatter_dimension=1, tiled=True),
        lax.psum_scatter(grad_down, ("shard", "ctx"), scatter_dimension=0, tiled=True),
    )
    total_gate, total_up, total_down = (
        lax.psum(owned_gate.astype(jnp.bfloat16), "rep").astype(jnp.float32),
        lax.psum(owned_up.astype(jnp.bfloat16), "rep").astype(jnp.float32),
        lax.psum(owned_down.astype(jnp.bfloat16), "rep").astype(jnp.float32),
    )
    d_mid = against_rows(d_gate, wg_full) + against_rows(d_up, wu_full)
    dg_mlp = jnp.sum(d_mid * mixed_in * scale_mid, axis=0)
    d_resid = grad_rows.astype(jnp.float32) + norm_backward(d_mid, mixed_in, scale_mid, g_mlp)
    residual_gradient_bfloat = d_resid.astype(jnp.bfloat16)
    grad_output = over_tokens(attention_output, residual_gradient_bfloat)
    attention_gradient = (
        against_rows(residual_gradient_bfloat, wo_full)
        .astype(jnp.bfloat16)
        .reshape(sequence_count, local_length, KEY_VALUE_HEADS, group_width, HEAD_DIM)
    )
    attention_heads = attention_output.reshape(
        sequence_count, local_length, KEY_VALUE_HEADS, group_width, HEAD_DIM
    )
    row_delta = jnp.sum(
        attention_gradient.astype(jnp.float32) * attention_heads.astype(jnp.float32), axis=-1
    )
    row_delta = jnp.transpose(row_delta, (0, 2, 3, 1))
    scores_again = (
        jnp.einsum("bqkgd,bskd->bkgqs", query_group, keys_all, preferred_element_type=jnp.float32)
        * score_scale
    )
    probs_back = jnp.where(allowed, jnp.exp(scores_again - log_total[..., None]), 0.0)
    probs_round = probs_back.astype(jnp.bfloat16)
    values_gradient = jnp.einsum(
        "bkgqs,bqkgd->bskd", probs_round, attention_gradient, preferred_element_type=jnp.float32
    )
    d_probs = jnp.einsum(
        "bqkgd,bskd->bkgqs", attention_gradient, values_all, preferred_element_type=jnp.float32
    )
    d_scores = (probs_back * (d_probs - row_delta[..., None])).astype(jnp.bfloat16)
    d_qrot = (
        jnp.einsum("bkgqs,bskd->bqkgd", d_scores, keys_all, preferred_element_type=jnp.float32)
        * score_scale
    )
    d_krot = (
        jnp.einsum("bkgqs,bqkgd->bskd", d_scores, query_group, preferred_element_type=jnp.float32)
        * score_scale
    )
    d_keys, value_rows_gradient = (
        lax.psum_scatter(
            d_krot.astype(jnp.bfloat16), "ctx", scatter_dimension=1, tiled=True
        ).astype(jnp.float32),
        lax.psum_scatter(
            values_gradient.astype(jnp.bfloat16), "ctx", scatter_dimension=1, tiled=True
        ).astype(jnp.float32),
    )
    d_qn = rotate_back(
        d_qrot.reshape(sequence_count, local_length, QUERY_HEADS, HEAD_DIM), cosine, sine
    )
    normed_key_gradient = rotate_back(d_keys, cosine, sine)
    dg_query = jnp.sum(d_qn * query * q_scale, axis=(0, 1, 2))
    dg_key = jnp.sum(normed_key_gradient * key_rows * key_scale, axis=(0, 1, 2))
    d_query = (
        norm_backward(d_qn, query, q_scale, g_query)
        .astype(jnp.bfloat16)
        .reshape(total_rows, QUERY_HEADS * HEAD_DIM)
    )
    key_gradient = (
        norm_backward(normed_key_gradient, key_rows, key_scale, key_gain)
        .astype(jnp.bfloat16)
        .reshape(total_rows, KEY_VALUE_HEADS * HEAD_DIM)
    )
    value_gradient = value_rows_gradient.astype(jnp.bfloat16).reshape(
        total_rows, KEY_VALUE_HEADS * HEAD_DIM
    )
    grad_query = over_tokens(normed_input, d_query)
    grad_key = over_tokens(normed_input, key_gradient)
    grad_value = over_tokens(normed_input, value_gradient)
    d_in = (
        against_rows(d_query, wq_full)
        + against_rows(key_gradient, full_key_weight)
        + against_rows(value_gradient, full_value_weight)
    )
    dg_attn = jnp.sum(d_in * x_rows * scale_in, axis=0)
    grad_input = (d_resid + norm_backward(d_in, x_rows, scale_in, g_attn)).reshape(
        sequence_count, local_length, model_width
    )
    grad_gains = jnp.concatenate([dg_attn, dg_query, dg_key, dg_mlp])
    owned_query, owned_key, owned_value, owned_output, owned_gains = (
        lax.psum_scatter(grad_query, ("shard", "ctx"), scatter_dimension=1, tiled=True),
        lax.psum_scatter(grad_key, ("shard", "ctx"), scatter_dimension=1, tiled=True),
        lax.psum_scatter(grad_value, ("shard", "ctx"), scatter_dimension=1, tiled=True),
        lax.psum_scatter(grad_output, ("shard", "ctx"), scatter_dimension=0, tiled=True),
        lax.psum_scatter(grad_gains, ("shard", "ctx"), scatter_dimension=0, tiled=True),
    )
    total_query, total_key, total_value, total_output, total_gains = (
        lax.psum(owned_query.astype(jnp.bfloat16), "rep").astype(jnp.float32),
        lax.psum(owned_key.astype(jnp.bfloat16), "rep").astype(jnp.float32),
        lax.psum(owned_value.astype(jnp.bfloat16), "rep").astype(jnp.float32),
        lax.psum(owned_output.astype(jnp.bfloat16), "rep").astype(jnp.float32),
        lax.psum(owned_gains.astype(jnp.bfloat16), "rep").astype(jnp.float32),
    )
    return (
        block_out,
        grad_input,
        total_query,
        total_key,
        total_value,
        total_output,
        total_gate,
        total_up,
        total_down,
        total_gains,
    )


def solution(mesh):
    in_specs = (
        P(("rep", "shard"), "ctx", None),
        P(("rep", "shard"), None),
        P(("rep", "shard"), None),
        P(("rep", "shard"), "ctx", None),
        P(None, ("shard", "ctx")),
        P(None, ("shard", "ctx")),
        P(None, ("shard", "ctx")),
        P(("shard", "ctx"), None),
        P(None, ("shard", "ctx")),
        P(None, ("shard", "ctx")),
        P(("shard", "ctx"), None),
        P(("shard", "ctx")),
    )
    out_specs = (
        P(("rep", "shard"), "ctx", None),
        P(("rep", "shard"), "ctx", None),
        P(None, ("shard", "ctx")),
        P(None, ("shard", "ctx")),
        P(None, ("shard", "ctx")),
        P(("shard", "ctx"), None),
        P(None, ("shard", "ctx")),
        P(None, ("shard", "ctx")),
        P(("shard", "ctx"), None),
        P(("shard", "ctx")),
    )
    return jax.shard_map(body, mesh=mesh, in_specs=in_specs, out_specs=out_specs, check_vma=False)
```

profile of v0, /device:TPU:0, one launch (start us, length us, event | category | flops | bytes accessed | tf_op | source)
XLA Modules:
  0.0 1393.0 jit_solution(7887829334335349230)
XLA Ops:
  12.3 36.6 %all-reduce = bf16[2304]{0:T(1024)(128)(2,1)S(1)} all-reduce(bf16[2304]{0:T(1024)(128)(2,1)S(1)} %dynamic-update-slice), channel_id=1, replica_groups=mesh['rep'=2,'shard'=4,'ctx'=4] {'shard','ctx'}, use_global_device_ids=true, to_apply=%add | all-reduce | flops 2304 | bytes 9216
  59.3 37.8 %all-gather.10.cloned.1.call-done = bf16[1024,1024]{0,1:T(8,128)(2,1)} async-done(((bf16[1024,64]{0,1:T(8,128)(2,1)}), bf16[1024,1024]{0,1:T(8,128)(2,1)}) %all-gather.10.cloned.1.call-update) | async-done | bytes 2097168 | tf_op jit(solution)/shard_map/all_gather | solution.py:92
  103.5 47.0 %all-gather.18.cloned.1.call-done = bf16[1024,2048]{1,0:T(8,128)(2,1)} async-done(((bf16[1024,128]{1,0:T(8,128)(2,1)}), bf16[1024,2048]{1,0:T(8,128)(2,1)}) %all-gather.18.cloned.1.call-update) | async-done | bytes 4194320 | tf_op jit(solution)/shard_map/all_gather | solution.py:90
  150.5 6.6 copy.36
  157.0 4.0 multiply_reduce_fusion.3
  161.9 16.8 %all-gather.16.cloned.1.call-done = bf16[2,256,8,128]{3,1,2,0:T(8,128)(2,1)} async-done(((bf16[2,64,8,128]{3,1,2,0:T(8,128)(2,1)}), bf16[2,256,8,128]{3,1,2,0:T(8,128)(2,1)}) %all-gather.16.cloned.1.call-update) | async-done | bytes 1048592 | tf_op jit(solution)/shard_map/all_gather | solution.py:121
  178.6 3.2 fusion.6
  182.5 25.5 %all-gather.12.cloned.1.call-done = bf16[2,256,8,128]{3,1,2,0:T(8,128)(2,1)} async-done(((bf16[2,64,8,128]{3,1,2,0:T(8,128)(2,1)}), bf16[2,256,8,128]{3,1,2,0:T(8,128)(2,1)}) %all-gather.12.cloned.1.call-update) | async-done | bytes 1048592 | tf_op jit(solution)/shard_map/all_gather | solution.py:122
  212.3 47.5 %all-gather.20.cloned.1.call-done = bf16[2048,1024]{1,0:T(8,128)(2,1)} async-done(((bf16[128,1024]{1,0:T(8,128)(2,1)}), bf16[2048,1024]{1,0:T(8,128)(2,1)}) %all-gather.20.cloned.1.call-update) | async-done | bytes 4194320 | tf_op jit(solution)/shard_map/all_gather | solution.py:93
  263.8 58.3 %all-gather.24.cloned.1.call-done = bf16[1024,3072]{0,1:T(8,128)(2,1)} async-done(((bf16[1024,192]{0,1:T(8,128)(2,1)}), bf16[1024,3072]{0,1:T(8,128)(2,1)}) %all-gather.24.cloned.1.call-update) | async-done | bytes 6291472 | tf_op jit(solution)/shard_map/all_gather | solution.py:150
  322.1 6.1 fusion.75
  328.3 56.3 %all-gather.22.cloned.1.call-done = bf16[1024,3072]{0,1:T(8,128)(2,1)} async-done(((bf16[1024,192]{0,1:T(8,128)(2,1)}), bf16[1024,3072]{0,1:T(8,128)(2,1)}) %all-gather.22.cloned.1.call-update) | async-done | bytes 6291472 | tf_op jit(solution)/shard_map/all_gather | solution.py:149
  384.6 6.4 fusion.74
  391.0 56.1 %all-gather.26.cloned.1.call-done = bf16[3072,1024]{1,0:T(8,128)(2,1)} async-done(((bf16[192,1024]{1,0:T(8,128)(2,1)}), bf16[3072,1024]{1,0:T(8,128)(2,1)}) %all-gather.26.cloned.1.call-update) | async-done | bytes 6291472 | tf_op jit(solution)/shard_map/all_gather | solution.py:151
  447.1 7.3 multiply_convert_fusion
  469.9 21.8 %reduce-scatter.10.cloned.1.call-done = bf16[2,64,8,128]{3,1,2,0:T(8,128)(2,1)} async-done(((bf16[2,256,8,128]{3,1,2,0:T(8,128)(2,1)}), bf16[2,64,8,128]{3,1,2,0:T(8,128)(2,1)}) %reduce-scatter.10.cloned.1.call-update) | async-done | bytes 262160 | tf_op jit(solution)/shard_map/reduce_scatter | solution.py:217
  498.2 21.6 %reduce-scatter.12.cloned.1.call-done = bf16[2,64,8,128]{3,2,0,1:T(8,128)(2,1)} async-done(((bf16[2,256,8,128]{3,2,0,1:T(8,128)(2,1)}), bf16[2,64,8,128]{3,2,0,1:T(8,128)(2,1)}) %reduce-scatter.12.cloned.1.call-update) | async-done | bytes 262160 | tf_op jit(solution)/shard_map/reduce_scatter | solution.py:220
  524.6 4.6 fusion.61
  535.4 4.6 fusion.25
  541.3 6.4 fusion.78
  548.8 6.4 fusion.77
  556.4 6.4 fusion.79
  563.6 31.2 %reduce-scatter.16.cloned.1.call-done = f32[1024,64]{0,1:T(8,128)} async-done(((f32[1024,1024]{0,1:T(8,128)}), f32[1024,64]{0,1:T(8,128)}) %reduce-scatter.16.cloned.1.call-update) | async-done | bytes 262160 | tf_op jit(solution)/shard_map/reduce_scatter | solution.py:258
  596.4 74.2 %reduce-scatter.18.cloned.1.call-done = f32[1024,64]{0,1:T(8,128)} async-done(((f32[1024,1024]{0,1:T(8,128)}), f32[1024,64]{0,1:T(8,128)}) %reduce-scatter.18.cloned.1.call-update) | async-done | bytes 262160 | tf_op jit(solution)/shard_map/reduce_scatter | solution.py:259
  672.2 104.8 %reduce-scatter.20.cloned.1.call-done = f32[128,1024]{1,0:T(8,128)} async-done(((f32[2048,1024]{1,0:T(8,128)}), f32[128,1024]{1,0:T(8,128)}) %reduce-scatter.20.cloned.1.call-update) | async-done | bytes 524304 | tf_op jit(solution)/shard_map/reduce_scatter | solution.py:260
  778.8 105.4 %reduce-scatter.14.cloned.1.call-done = f32[1024,128]{1,0:T(8,128)} async-done(((f32[1024,2048]{1,0:T(8,128)}), f32[1024,128]{1,0:T(8,128)}) %reduce-scatter.14.cloned.1.call-update) | async-done | bytes 524304 | tf_op jit(solution)/shard_map/reduce_scatter | solution.py:257
  885.9 136.7 %reduce-scatter.24.cloned.1.call-done = f32[1024,192]{0,1:T(8,128)} async-done(((f32[1024,3072]{0,1:T(8,128)}), f32[1024,192]{0,1:T(8,128)}) %reduce-scatter.24.cloned.1.call-update) | async-done | bytes 786448 | tf_op jit(solution)/shard_map/reduce_scatter | solution.py:170
  1024.6 136.2 %reduce-scatter.22.cloned.1.call-done = f32[1024,192]{0,1:T(8,128)} async-done(((f32[1024,3072]{0,1:T(8,128)}), f32[1024,192]{0,1:T(8,128)}) %reduce-scatter.22.cloned.1.call-update) | async-done | bytes 786448 | tf_op jit(solution)/shard_map/reduce_scatter | solution.py:169
  1162.7 136.2 %reduce-scatter.26.cloned.1.call-done = f32[192,1024]{1,0:T(8,128)} async-done(((f32[3072,1024]{1,0:T(8,128)}), f32[192,1024]{1,0:T(8,128)}) %reduce-scatter.26.cloned.1.call-update) | async-done | bytes 786448 | tf_op jit(solution)/shard_map/reduce_scatter | solution.py:171
  1300.9 4.6 fusion.12
  1309.9 59.7 %all-reduce.1 = bf16[2304]{0:T(1024)(128)(2,1)S(1)} all-reduce(f32[2304]{0:T(1024)S(1)} %pad_maximum_fusion.6), channel_id=11, replica_groups=mesh['rep'=2,'shard'=4,'ctx'=4] {'shard','ctx'}, use_global_device_ids=true, to_apply=%region_30.31.clone | all-reduce | flops 2304 | bytes 13824
  1369.7 4.9 psum.63
  (244 shorter events, 95.3 us)
Async XLA Ops:
  7.2 47.5 %all-gather.14.cloned.1.call-start = ((), (), s32[]{:S(2)}) async-start(), calls=%async_computation.11 | async-start | bytes 2228224 | tf_op jit(solution)/shard_map/all_gather | solution.py:91
  7.9 89.2 %all-gather.10.cloned.1.call-start = ((), (), s32[]{:S(2)}) async-start(), calls=%async_computation.9 | async-start | bytes 2228224 | tf_op jit(solution)/shard_map/all_gather | solution.py:92
  8.7 141.8 %all-gather.18.cloned.1.call-start = ((), (), s32[]{:S(2)}) async-start(), calls=%async_computation.13 | async-start | bytes 4456448 | tf_op jit(solution)/shard_map/all_gather | solution.py:90
  9.4 169.3 %all-gather.16.cloned.1.call-start = ((), (), s32[]{:S(2)}) async-start(), calls=%async_computation.12 | async-start | bytes 1310720 | tf_op jit(solution)/shard_map/all_gather | solution.py:121
  50.7 110.3 %copy-start.50 = (f32[128]{0:T(128)}, f32[128]{0:T(128)S(1)}, u32[]{:S(2)}) copy-start(f32[128]{0:T(128)S(1)} %get-tuple-element.40) | copy-start | bytes 1540
  50.8 212.1 %copy-start.44 = (f32[1024]{0:T(1024)}, f32[1024]{0:T(1024)S(1)}, u32[]{:S(2)}) copy-start(f32[1024]{0:T(1024)S(1)} %get-tuple-element.38) | copy-start | bytes 12292
  59.0 149.0 %all-gather.12.cloned.1.call-start = ((), (), s32[]{:S(2)}) async-start(), calls=%async_computation.10 | async-start | bytes 1310720 | tf_op jit(solution)/shard_map/all_gather | solution.py:122
  59.1 41.2 %copy-start.54 = (f32[128]{0:T(128)}, f32[128]{0:T(128)S(1)}, u32[]{:S(2)}) copy-start(f32[128]{0:T(128)S(1)} %rsqrt.37) | copy-start | bytes 1540
  59.3 44.0 %copy-start.57 = (s32[2,256]{1,0:T(2,128)S(1)}, s32[2,256]{1,0:T(2,128)}, u32[]{:S(2)}) copy-start(s32[2,256]{1,0:T(2,128)} %param.14) | copy-start | bytes 6148
  59.3 44.1 %copy-start.56 = (s32[2,256]{1,0:T(2,128)S(1)}, s32[2,256]{1,0:T(2,128)}, u32[]{:S(2)}) copy-start(s32[2,256]{1,0:T(2,128)} %param.13) | copy-start | bytes 6148
  100.4 159.5 %all-gather.20.cloned.1.call-start = ((), (), s32[]{:S(2)}) async-start(), calls=%async_computation.14 | async-start | bytes 4456448 | tf_op jit(solution)/shard_map/all_gather | solution.py:93
  101.0 221.2 %all-gather.24.cloned.1.call-start = ((), (), s32[]{:S(2)}) async-start(), calls=%async_computation.16 | async-start | bytes 6684672 | tf_op jit(solution)/shard_map/all_gather | solution.py:150
  101.7 282.9 %all-gather.22.cloned.1.call-start = ((), (), s32[]{:S(2)}) async-start(), calls=%async_computation.15 | async-start | bytes 6684672 | tf_op jit(solution)/shard_map/all_gather | solution.py:149
  102.5 344.6 %all-gather.26.cloned.1.call-start = ((), (), s32[]{:S(2)}) async-start(), calls=%async_computation.17 | async-start | bytes 6684672 | tf_op jit(solution)/shard_map/all_gather | solution.py:151
  103.2 388.4 %reduce-scatter.10.cloned.1.call-start = ((), (), s32[]{:S(2)}) async-start(), calls=%async_computation.18 | async-start | bytes 1310720 | tf_op jit(solution)/shard_map/reduce_scatter | solution.py:217
  103.5 104.6 %copy-start.46 = (pred[2,64,256]{2,1,0:T(8,128)(4,1)}, pred[2,64,256]{2,1,0:T(8,128)(4,1)S(1)}, u32[]{:S(2)}) copy-start(pred[2,64,256]{2,1,0:T(8,128)(4,1)S(1)} %compare_and_fusion) | copy-start | bytes 98308
  161.8 20.0 %copy-start.27 = (bf16[2,64,16,64]{3,1,2,0:T(8,128)(2,1)}, bf16[2,64,16,64]{3,1,2,0:T(8,128)(2,1)S(1)}, u32[]{:S(2)}) copy-start(bf16[2,64,16,64]{3,1,2,0:T(8,128)(2,1)S(1)} %get-tuple-element.32) | copy-start | bytes 786436
  212.3 50.5 %copy-start.18 = (bf16[128,2048]{1,0:T(8,128)(2,1)}, bf16[128,2048]{1,0:T(8,128)(2,1)S(1)}, u32[]{:S(2)}) copy-start(bf16[128,2048]{1,0:T(8,128)(2,1)S(1)} %reshape.196) | copy-start | bytes 1572868
  262.9 65.4 %copy-start.52 = (f32[128]{0:T(128)}, f32[128]{0:T(128)S(1)}, u32[]{:S(2)}) copy-start(f32[128]{0:T(128)S(1)} %add_rsqrt_fusion.3) | copy-start | bytes 1540
  263.8 64.5 %copy-start.12 = (bf16[128,1024]{1,0:T(8,128)(2,1)}, bf16[128,1024]{1,0:T(8,128)(2,1)S(1)}, u32[]{:S(2)}) copy-start(bf16[128,1024]{1,0:T(8,128)(2,1)S(1)} %multiply_convert_fusion.5) | copy-start | bytes 786436
  384.6 70.9 %slice-start = ((s8[6291456]{0:T(1024)(128)(4,1)}), s8[2097152]{0:T(1024)(128)(4,1)S(1)}, s32[]{:S(2)}) async-start(s8[6291456]{0:T(1024)(128)(4,1)} %bitcast.176), calls=%async_computation.28 | async-start | bytes 4194304
  465.5 54.3 %reduce-scatter.12.cloned.1.call-start = ((), (), s32[]{:S(2)}) async-start(), calls=%async_computation.19 | async-start | bytes 1310720 | tf_op jit(solution)/shard_map/reduce_scatter | solution.py:220
  469.8 23.2 %copy-start.11 = (f32[2,64,8,128]{3,1,2,0:T(8,128)S(1)}, f32[2,64,8,128]{3,1,2,0:T(8,128)}, u32[]{:S(2)}) copy-start(f32[2,64,8,128]{3,1,2,0:T(8,128)} %copy-done.10) | copy-start | bytes 1572868
  469.8 125.0 %reduce-scatter.16.cloned.1.call-start = ((), (), s32[]{:S(2)}) async-start(), calls=%async_computation.21 | async-start | bytes 4456448 | tf_op jit(solution)/shard_map/reduce_scatter | solution.py:258
  498.1 172.4 %reduce-scatter.18.cloned.1.call-start = ((), (), s32[]{:S(2)}) async-start(), calls=%async_computation.22 | async-start | bytes 4456448 | tf_op jit(solution)/shard_map/reduce_scatter | solution.py:259
  523.6 253.4 %reduce-scatter.20.cloned.1.call-start = ((), (), s32[]{:S(2)}) async-start(), calls=%async_computation.23 | async-start | bytes 8912896 | tf_op jit(solution)/shard_map/reduce_scatter | solution.py:260
  529.2 354.9 %reduce-scatter.14.cloned.1.call-start = ((), (), s32[]{:S(2)}) async-start(), calls=%async_computation.20 | async-start | bytes 8912896 | tf_op jit(solution)/shard_map/reduce_scatter | solution.py:257
  540.1 482.6 %reduce-scatter.24.cloned.1.call-start = ((), (), s32[]{:S(2)}) async-start(), calls=%async_computation.25 | async-start | bytes 13369344 | tf_op jit(solution)/shard_map/reduce_scatter | solution.py:170
  547.7 613.0 %reduce-scatter.22.cloned.1.call-start = ((), (), s32[]{:S(2)}) async-start(), calls=%async_computation.24 | async-start | bytes 13369344 | tf_op jit(solution)/shard_map/reduce_scatter | solution.py:169
  555.3 743.6 %reduce-scatter.26.cloned.1.call-start = ((), (), s32[]{:S(2)}) async-start(), calls=%async_computation.26 | async-start | bytes 13369344 | tf_op jit(solution)/shard_map/reduce_scatter | solution.py:171
  562.9 813.3 %all-reduce.5.cloned.1.call-start = ((), (), s32[]{:S(2)}) async-start(), calls=%async_computation.27 | async-start | bytes 3932160 | tf_op jit(solution)/shard_map/psum | solution.py:264
  1024.6 276.2 %copy-start.5 = (f32[128,1024]{1,0:T(8,128)S(1)}, f32[128,1024]{1,0:T(8,128)}, u32[]{:S(2)}) copy-start(f32[128,1024]{1,0:T(8,128)} %copy-done.3) | copy-start | bytes 1572868
  (48 other events, 152.1 us)
Sparse Core Ops, SparseCore 0:
  10.2 44.4 all-gather.13
  56.9 40.2 all-gather.9
  99.2 51.1 all-gather.17
  152.5 26.1 all-gather.15
  180.6 27.3 all-gather.11
  210.1 49.7 all-gather.19
  262.2 59.9 all-gather.23
  324.4 60.1 all-gather.21
  386.9 60.0 all-gather.25
  465.6 25.9 reduce-scatter.9
  493.9 25.7 reduce-scatter.11
  523.5 71.2 reduce-scatter.15
  598.7 71.8 reduce-scatter.17
  674.5 102.4 reduce-scatter.19
  780.9 103.1 reduce-scatter.13
  888.1 134.5 reduce-scatter.23
  1026.5 134.1 reduce-scatter.21
  1164.6 134.1 reduce-scatter.25
  1302.7 59.4 all-reduce.4
where the time goes:
time: 1400 us; the launch traced here: 1390 us
  waiting for transfers between devices  1120 us (80%)
  blocking collectives  101 us (7%)
  matrix products  91.9 us (7%)
  other arithmetic  36.6 us (3%)
  local copies, waits for them, and re-layouts  25.3 us (2%)
  between operations  16.6 us (1%)
    reduce_scatter x1, waiting for transfers between devices, body(): lax.psum_scatter(grad_up, ('shard', 'ctx'), scatter_dimension=1, tiled=True)  137 us
    reduce_scatter x1, waiting for transfers between devices, body(): lax.psum_scatter(grad_down, ('shard', 'ctx'), scatter_dimension=0, tiled=...  136 us
    reduce_scatter x1, waiting for transfers between devices, body(): lax.psum_scatter(grad_gate, ('shard', 'ctx'), scatter_dimension=1, tiled=...  136 us
    reduce_scatter x1, waiting for transfers between devices, body(): lax.psum_scatter(grad_query, ('shard', 'ctx'), scatter_dimension=1, tiled...  105 us
    reduce_scatter x1, waiting for transfers between devices, body(): lax.psum_scatter(grad_output, ('shard', 'ctx'), scatter_dimension=0, tile...  105 us
    unnamed x2, blocking collectives  96.3 us
    reduce_scatter x1, waiting for transfers between devices, body(): lax.psum_scatter(grad_value, ('shard', 'ctx'), scatter_dimension=1, tiled...  74.2 us
    all_gather x1, waiting for transfers between devices, body(): lax.all_gather(w_up, ('shard', 'ctx'), axis=1, tiled=True)  58.3 us
  transfers between devices with their start and end apart: 19, of which 18 were waited for; matrix products, arithmetic and copies ran while one was open for 8% of the time, Pallas kernels for 0%

commit v1 on v0

--- a/solution.py
+++ b/solution.py
@@ -281,6 +281,234 @@
     )
 
 
+def gather_ctx(rows_in):
+    return lax.all_gather(rows_in, "ctx", axis=1, tiled=True)
+
+
+def scatter_ctx(partial, sequence_count):
+    total_rows, width = partial.shape
+    shaped = partial.astype(jnp.bfloat16).reshape(sequence_count, total_rows // sequence_count, width)
+    owned = lax.psum_scatter(shaped, "ctx", scatter_dimension=1, tiled=True)
+    return owned.astype(jnp.float32).reshape(-1, width)
+
+
+def gather_columns(block):
+    gathered = lax.all_gather(block, "shard", axis=0, tiled=False)
+    return jnp.transpose(gathered, (1, 0, 2))
+
+
+def finish(owned):
+    return lax.psum(owned.astype(jnp.bfloat16), "rep").astype(jnp.float32)
+
+
+def head_parallel_body(
+    tokens,
+    positions,
+    segments,
+    cotangent,
+    w_query,
+    key_weight,
+    value_weight,
+    output_weight,
+    w_gate,
+    w_up,
+    w_down,
+    norm_gains,
+):
+    sequence_count, local_length, model_width = tokens.shape
+    context_size = lax.axis_size("ctx")
+    shard_size = lax.axis_size("shard")
+    full_length = local_length * context_size
+    half_width = key_weight.shape[1]
+    ff_width = w_gate.shape[1]
+    heads = shard_size
+    score_scale = 1.0 / math.sqrt(HEAD_DIM)
+    odd = lax.rem(lax.axis_index("ctx"), 2) == 1
+    partners = [(i, i + 1 - 2 * (i % 2)) for i in range(context_size)]
+
+    own_kv = jnp.concatenate([key_weight, value_weight], axis=1)
+    peer_kv = lax.ppermute(own_kv, "ctx", partners)
+    low = jnp.where(odd, peer_kv, own_kv)
+    high = jnp.where(odd, own_kv, peer_kv)
+    qkv_block = jnp.concatenate(
+        [
+            w_query,
+            low[:, :half_width],
+            high[:, :half_width],
+            low[:, half_width:],
+            high[:, half_width:],
+        ],
+        axis=1,
+    )
+    x_all = gather_ctx(tokens)
+    gain_all = lax.all_gather(norm_gains, ("shard", "ctx"), axis=0, tiled=True).astype(jnp.float32)
+    qkv_full = gather_columns(qkv_block)
+    wo_full = lax.all_gather(output_weight, "shard", axis=0, tiled=True)
+    gu_full = gather_columns(jnp.concatenate([w_gate, w_up], axis=1)).reshape(model_width, -1)
+    wd_full = lax.all_gather(w_down, "shard", axis=0, tiled=True)
+    grad_all = gather_ctx(cotangent).reshape(-1, model_width)
+
+    wq_full = qkv_full[:, :, :HEAD_DIM].reshape(model_width, -1)
+    wk_full = qkv_full[:, :, HEAD_DIM : 2 * HEAD_DIM].reshape(model_width, -1)
+    wv_full = qkv_full[:, :, 2 * HEAD_DIM :].reshape(model_width, -1)
+    g_attn = gain_all[:model_width]
+    g_query = gain_all[model_width : model_width + HEAD_DIM]
+    key_gain = gain_all[model_width + HEAD_DIM : model_width + 2 * HEAD_DIM]
+    g_mlp = gain_all[model_width + 2 * HEAD_DIM :]
+
+    x_full = x_all.reshape(-1, model_width).astype(jnp.float32)
+    normed_input = (x_full * rms_scale(x_full) * g_attn).astype(jnp.bfloat16)
+    head_shape = (sequence_count, full_length, heads, HEAD_DIM)
+    query = float_product(normed_input, wq_full).reshape(head_shape)
+    key_rows = float_product(normed_input, wk_full).reshape(head_shape)
+    value_rows = float_product(normed_input, wv_full).astype(jnp.bfloat16).reshape(head_shape)
+    q_scale = rms_scale(query)
+    key_scale = rms_scale(key_rows)
+    cosine, sine = rope_tables(positions)
+    q_rot = rotate(query * q_scale * g_query, cosine, sine).astype(jnp.bfloat16)
+    k_rot = rotate(key_rows * key_scale * key_gain, cosine, sine).astype(jnp.bfloat16)
+    allowed = (
+        (segments[:, :, None] == segments[:, None, :])
+        & (positions[:, None, :] <= positions[:, :, None])
+    )[:, None]
+    scores = (
+        jnp.einsum("bqhd,bshd->bhqs", q_rot, k_rot, preferred_element_type=jnp.float32)
+        * score_scale
+    )
+    exponent = jnp.where(allowed, jnp.exp(scores), 0.0)
+    denominator = jnp.sum(exponent, axis=-1, keepdims=True)
+    probs = exponent / denominator
+    probs_round = probs.astype(jnp.bfloat16)
+    attended = (
+        jnp.einsum("bhqs,bshd->bqhd", probs_round, value_rows, preferred_element_type=jnp.float32)
+        .astype(jnp.bfloat16)
+    )
+    attended_rows = attended.reshape(-1, heads * HEAD_DIM)
+    x_rows = tokens.reshape(-1, model_width).astype(jnp.float32)
+    mixed_in = x_rows + scatter_ctx(float_product(attended_rows, wo_full), sequence_count)
+    scale_mid = rms_scale(mixed_in)
+    local_shape = tokens.shape
+    normed_mid = gather_ctx(
+        (mixed_in * scale_mid * g_mlp).astype(jnp.bfloat16).reshape(local_shape)
+    ).reshape(-1, model_width)
+
+    d_hidden = against_rows(grad_all, wd_full)
+    gate_up = float_product(normed_mid, gu_full).reshape(-1, shard_size, 2 * ff_width)
+    gate_pre = gate_up[:, :, :ff_width].reshape(-1, shard_size * ff_width)
+    up_pre = gate_up[:, :, ff_width:].reshape(-1, shard_size * ff_width)
+    sigmoid_gate = jax.nn.sigmoid(gate_pre)
+    hidden = (gate_pre * sigmoid_gate * up_pre).astype(jnp.bfloat16)
+    d_gate = (d_hidden * up_pre * sigmoid_gate * (1.0 + gate_pre * (1.0 - sigmoid_gate))).astype(
+        jnp.bfloat16
+    )
+    d_up = (d_hidden * gate_pre * sigmoid_gate).astype(jnp.bfloat16)
+    d_gu = jnp.concatenate(
+        [
+            d_gate.reshape(-1, shard_size, ff_width),
+            d_up.reshape(-1, shard_size, ff_width),
+        ],
+        axis=2,
+    ).reshape(-1, 2 * shard_size * ff_width)
+    d_mid = scatter_ctx(against_rows(d_gu, gu_full), sequence_count)
+    grad_rows = cotangent.reshape(-1, model_width)
+    dg_mlp = jnp.sum(d_mid * mixed_in * scale_mid, axis=0)
+    d_resid = grad_rows.astype(jnp.float32) + norm_backward(d_mid, mixed_in, scale_mid, g_mlp)
+    resid_all = gather_ctx(d_resid.astype(jnp.bfloat16).reshape(local_shape)).reshape(
+        -1, model_width
+    )
+
+    block_sum = mixed_in + scatter_ctx(float_product(hidden, wd_full), sequence_count)
+    block_out = block_sum.astype(jnp.bfloat16).reshape(local_shape)
+    grad_gu = over_tokens(normed_mid, d_gu).astype(jnp.bfloat16)
+    grad_gu = grad_gu.reshape(model_width, shard_size, 2 * ff_width)
+    owned_gu = lax.psum_scatter(
+        jnp.transpose(grad_gu, (1, 0, 2)), "shard", scatter_dimension=0, tiled=False
+    )
+    grad_down = over_tokens(hidden, grad_all).astype(jnp.bfloat16)
+    owned_down = lax.psum_scatter(grad_down, "shard", scatter_dimension=0, tiled=True)
+    total_gu, total_down = finish(owned_gu), finish(owned_down)
+
+    d_att = against_rows(resid_all, wo_full).astype(jnp.bfloat16).reshape(head_shape)
+    grad_output = over_tokens(attended_rows, resid_all).astype(jnp.bfloat16)
+    row_delta = jnp.sum(d_att.astype(jnp.float32) * attended.astype(jnp.float32), axis=-1)
+    row_delta = jnp.transpose(row_delta, (0, 2, 1))[..., None]
+    d_values = jnp.einsum("bhqs,bqhd->bshd", probs_round, d_att, preferred_element_type=jnp.float32)
+    d_probs = jnp.einsum("bqhd,bshd->bhqs", d_att, value_rows, preferred_element_type=jnp.float32)
+    d_scores = (probs * (d_probs - row_delta)).astype(jnp.bfloat16)
+    d_qrot = (
+        jnp.einsum("bhqs,bshd->bqhd", d_scores, k_rot, preferred_element_type=jnp.float32)
+        * score_scale
+    )
+    d_krot = (
+        jnp.einsum("bhqs,bqhd->bshd", d_scores, q_rot, preferred_element_type=jnp.float32)
+        * score_scale
+    )
+    d_qn = rotate_back(d_qrot, cosine, sine)
+    d_kn = rotate_back(d_krot, cosine, sine)
+    dg_query = jnp.sum(d_qn * query * q_scale, axis=(0, 1, 2))
+    dg_key = jnp.sum(d_kn * key_rows * key_scale, axis=(0, 1, 2))
+    d_query = norm_backward(d_qn, query, q_scale, g_query).astype(jnp.bfloat16)
+    d_query = d_query.reshape(-1, heads * HEAD_DIM)
+    d_key = norm_backward(d_kn, key_rows, key_scale, key_gain)
+    d_key_b = d_key.astype(jnp.bfloat16)
+    d_value_b = d_values.astype(jnp.bfloat16)
+    d_in_part = (
+        against_rows(d_query, wq_full)
+        + against_rows(d_key_b.reshape(-1, heads * HEAD_DIM), wk_full)
+        + against_rows(d_value_b.reshape(-1, heads * HEAD_DIM), wv_full)
+    )
+    kv_low = jnp.concatenate([d_key_b[..., :half_width], d_value_b[..., :half_width]], axis=-1)
+    kv_high = jnp.concatenate([d_key_b[..., half_width:], d_value_b[..., half_width:]], axis=-1)
+    kv_own = jnp.where(odd, kv_high, kv_low)
+    kv_other = lax.ppermute(jnp.where(odd, kv_low, kv_high), "ctx", partners)
+    kv_rows = (kv_own.astype(jnp.float32) + kv_other.astype(jnp.float32)).astype(jnp.bfloat16)
+    kv_rows = kv_rows.reshape(-1, heads * 2 * half_width)
+    d_in = scatter_ctx(d_in_part, sequence_count)
+    grad_query = over_tokens(normed_input, d_query).astype(jnp.bfloat16)
+    grad_kv = over_tokens(normed_input, kv_rows).astype(jnp.bfloat16)
+    grad_qkv = jnp.concatenate(
+        [
+            grad_query.reshape(model_width, shard_size, HEAD_DIM),
+            grad_kv.reshape(model_width, shard_size, 2 * half_width),
+        ],
+        axis=2,
+    )
+    owned_output = lax.psum_scatter(grad_output, "shard", scatter_dimension=0, tiled=True)
+    owned_qkv = lax.psum_scatter(
+        jnp.transpose(grad_qkv, (1, 0, 2)), "shard", scatter_dimension=0, tiled=False
+    )
+    total_output, total_qkv = finish(owned_output), finish(owned_qkv)
+    scale_in = rms_scale(x_rows)
+    dg_attn = jnp.sum(d_in * x_rows * scale_in, axis=0)
+    grad_input = (d_resid + norm_backward(d_in, x_rows, scale_in, g_attn)).reshape(local_shape)
+    grad_gains = jnp.concatenate([dg_attn, dg_query, dg_key, dg_mlp])
+    owned_gains = lax.psum_scatter(
+        grad_gains, ("shard", "ctx"), scatter_dimension=0, tiled=True
+    )
+    total_gains = finish(owned_gains)
+    return (
+        block_out,
+        grad_input,
+        total_qkv[:, :HEAD_DIM],
+        total_qkv[:, HEAD_DIM : HEAD_DIM + half_width],
+        total_qkv[:, HEAD_DIM + half_width :],
+        total_output,
+        total_gu[:, :ff_width],
+        total_gu[:, ff_width:],
+        total_down,
+        total_gains,
+    )
+
+
+def any_body(*arguments):
+    w_query, key_weight = arguments[4:6]
+    whole_query_head = w_query.shape[1] == HEAD_DIM
+    half_key_head = 2 * key_weight.shape[1] == HEAD_DIM
+    if whole_query_head and half_key_head and lax.axis_size("ctx") % 2 == 0:
+        return head_parallel_body(*arguments)
+    return body(*arguments)
+
+
 def solution(mesh):
     in_specs = (
         P(("rep", "shard"), "ctx", None),
@@ -308,4 +536,4 @@
         P(("shard", "ctx"), None),
         P(("shard", "ctx")),
     )
-    return jax.shard_map(body, mesh=mesh, in_specs=in_specs, out_specs=out_specs, check_vma=False)
+    return jax.shard_map(any_body, mesh=mesh, in_specs=in_specs, out_specs=out_specs, check_vma=False)

time: 1400 us -> 572 us (0.41)
  waiting for transfers between devices: 1120 us -> 319 us
  matrix products: 91.9 us -> 44.9 us
  local copies, waits for them, and re-layouts: 25.3 us -> 54 us
    reduce_scatter x9 -> x8, waiting for transfers between devices: 768 us -> 162 us  [the longest x4 82.5 us: scatter_ctx(): owned = lax.psum_scatter(shaped, 'ctx', scatter_dimension=1, tiled=True)]
    all_gather x9 -> x8, waiting for transfers between devices: 348 us -> 118 us  [the longest x4 64.6 us: gather_ctx(): return lax.all_gather(rows_in, 'ctx', axis=1, tiled=True)]
    psum x1, waiting for transfers between devices: 0.01 us -> 20.8 us  [finish(): return lax.psum(owned.astype(jnp.bfloat16), 'rep').astype(jnp.float32)]
    dot_general x7 -> x5, matrix products: 33.9 us -> 13.8 us  [over_tokens(): lax.dot_general(left, right, (((0,), (0,)), ((), ())), preferred_element_...]
    dot_general x7 -> x6, matrix products: 29 us -> 14 us  [float_product(): return jnp.dot(left, right, preferred_element_type=jnp.float32)]
    ppermute x0 -> x2, waiting for transfers between devices: none -> 14.7 us  [the longest x1 8.39 us: head_parallel_body(): kv_other = lax.ppermute(jnp.where(odd, kv_low, kv_high), 'ctx', partners)]
    convert_element_type x21 -> x10, other arithmetic: 27 us -> 12.7 us  [the longest x1 2.53 us: head_parallel_body(): normed_input = (x_full * rms_scale(x_full) * g_attn).astype(jnp.bfloat16)]
  transfers between devices with their start and end apart: 19 -> 19, of which waited for: 18 -> 16; matrix products, arithmetic and copies ran while one was open for 8% -> 16% of each run, Pallas kernels for 0% -> 0%
where the time goes in v1:
time: 572 us; the launch traced here: 570 us
  waiting for transfers between devices  319 us (56%)
  blocking collectives  99.7 us (17%)
  local copies, waits for them, and re-layouts  54 us (9%)
  matrix products  44.9 us (8%)
  other arithmetic  30.7 us (5%)
  between operations  16.3 us (3%)
  starting transfers between devices  5.97 us (1%)
    unnamed x2, blocking collectives  94.8 us
    reduce_scatter x4, waiting for transfers between devices, scatter_ctx(): owned = lax.psum_scatter(shaped, 'ctx', scatter_dimension=1, tiled=True)  82.5 us
    all_gather x4, waiting for transfers between devices, gather_ctx(): return lax.all_gather(rows_in, 'ctx', axis=1, tiled=True)  64.6 us
    reduce_scatter x1, waiting for transfers between devices, head_parallel_body(): lax.psum_scatter(jnp.transpose(grad_gu, (1, 0, 2)), 'shard', scatter_dime...  40.5 us
    reduce_scatter x1, waiting for transfers between devices, head_parallel_body(): lax.psum_scatter(jnp.transpose(grad_qkv, (1, 0, 2)), 'shard', scatter_dim...  33.6 us
    all_gather x2, waiting for transfers between devices, gather_columns(): gathered = lax.all_gather(block, 'shard', axis=0, tiled=False)  31 us
    psum x1, waiting for transfers between devices, finish(): return lax.psum(owned.astype(jnp.bfloat16), 'rep').astype(jnp.float32)  20.8 us
    all_gather x1, waiting for transfers between devices, head_parallel_body(): wd_full = lax.all_gather(w_down, 'shard', axis=0, tiled=True)  20.6 us
  transfers between devices with their start and end apart: 19, of which 16 were waited for; matrix products, arithmetic and copies ran while one was open for 16% of the time, Pallas kernels for 0%

profile of v1, /device:TPU:0, one launch (start us, length us, event | category | flops | bytes accessed | tf_op | source)
XLA Modules:
  0.0 570.4 jit_solution(15638928412723321463)
XLA Ops:
  10.3 3.1 collective-permute-start
  13.4 6.3 %collective-permute-done = bf16[1024,128]{1,0:T(8,128)(2,1)S(1)} collective-permute-done((bf16[1024,128]{1,0:T(8,128)(2,1)S(1)}, bf16[1024,128]{1,0:T(8,128)(2,1)S(1)}, u32[]{:S(2)}, u32[]{:S(2)}) %collective-permute-start) | collective-permute-done | bytes 262176 | tf_op jit(solution)/shard_map/ppermute | solution.py:330
  23.9 35.1 %all-reduce = bf16[2304]{0:T(1024)(128)(2,1)S(1)} all-reduce(bf16[2304]{0:T(1024)(128)(2,1)S(1)} %dynamic-update-slice), channel_id=1, replica_groups=mesh['rep'=2,'shard'=4,'ctx'=4] {'shard','ctx'}, use_global_device_ids=true, to_apply=%add | all-reduce | flops 2304 | bytes 9216
  65.1 6.6 %all-gather.23.cloned.1.call-done = bf16[4096,384]{1,0:T(8,128)(2,1)} async-done(((bf16[1024,384]{1,0:T(8,128)(2,1)}), bf16[4096,384]{1,0:T(8,128)(2,1)}) %all-gather.23.cloned.1.call-update) | async-done | bytes 3145744 | tf_op jit(solution)/shard_map/all_gather | solution.py:296
  71.7 3.0 fusion.62
  89.9 2.9 convolution_convert_fusion.6
  93.9 26.4 %reduce-scatter.9.cloned.1.call-done = bf16[2,64,1024]{2,1,0:T(8,128)(2,1)} async-done(((bf16[2,256,1024]{2,1,0:T(8,128)(2,1)}), bf16[2,64,1024]{2,1,0:T(8,128)(2,1)}) %reduce-scatter.9.cloned.1.call-update) | async-done | bytes 262160 | tf_op jit(solution)/shard_map/reduce_scatter | solution.py:291
  125.0 24.4 %all-gather.25.cloned.1.call-done = bf16[4096,384]{0,1:T(8,128)(2,1)} async-done(((bf16[1024,384]{0,1:T(8,128)(2,1)}), bf16[4096,384]{0,1:T(8,128)(2,1)}) %all-gather.25.cloned.1.call-update) | async-done | bytes 3145744 | tf_op jit(solution)/shard_map/all_gather | solution.py:296
  149.3 3.4 copy.167
  152.8 2.9 copy.168
  155.6 23.7 %all-gather.15.cloned.1.call-done = bf16[2,256,1024]{2,1,0:T(8,128)(2,1)} async-done(((bf16[2,64,1024]{2,1,0:T(8,128)(2,1)}), bf16[2,256,1024]{2,1,0:T(8,128)(2,1)}) %all-gather.15.cloned.1.call-update) | async-done | bytes 1048592 | tf_op jit(solution)/shard_map/all_gather | solution.py:285
  179.3 4.1 fusion
  185.7 3.1 copy.171
  188.8 3.0 copy.170
  191.8 16.5 %all-gather.19.cloned.1.call-done = bf16[2,256,1024]{2,1,0:T(8,128)(2,1)} async-done(((bf16[2,64,1024]{2,1,0:T(8,128)(2,1)}), bf16[2,256,1024]{2,1,0:T(8,128)(2,1)}) %all-gather.19.cloned.1.call-update) | async-done | bytes 1048592 | tf_op jit(solution)/shard_map/all_gather | solution.py:285
  208.3 20.6 %all-gather.17.cloned.1.call-done = bf16[768,1024]{1,0:T(8,128)(2,1)} async-done(((bf16[192,1024]{1,0:T(8,128)(2,1)}), bf16[768,1024]{1,0:T(8,128)(2,1)}) %all-gather.17.cloned.1.call-update) | async-done | bytes 1572880 | tf_op jit(solution)/shard_map/all_gather | solution.py:348
  228.9 5.2 multiply_convert_fusion.3
  248.2 27.4 %reduce-scatter.13.cloned.1.call-done = bf16[2,64,1024]{2,1,0:T(8,128)(2,1)} async-done(((bf16[2,256,1024]{2,1,0:T(8,128)(2,1)}), bf16[2,64,1024]{2,1,0:T(8,128)(2,1)}) %reduce-scatter.13.cloned.1.call-update) | async-done | bytes 262160 | tf_op jit(solution)/shard_map/reduce_scatter | solution.py:291
  281.9 24.4 %all-gather.21.cloned.1.call-done = bf16[2,256,1024]{2,1,0:T(8,128)(2,1)} async-done(((bf16[2,64,1024]{2,1,0:T(8,128)(2,1)}), bf16[2,256,1024]{2,1,0:T(8,128)(2,1)}) %all-gather.21.cloned.1.call-update) | async-done | bytes 1048592 | tf_op jit(solution)/shard_map/all_gather | solution.py:285
  306.3 2.9 convolution_convert_fusion.3
  311.2 3.6 convolution_convert_fusion
  314.8 2.9 copy.202
  331.3 2.9 convolution_convert_fusion.5
  334.3 8.4 %collective-permute-done.1 = bf16[2,256,4,128]{1,3,2,0:T(8,128)(2,1)} collective-permute-done((bf16[2,256,4,128]{1,3,2,0:T(8,128)(2,1)}, bf16[2,256,4,128]{1,3,2,0:T(8,128)(2,1)}, u32[]{:S(2)}, u32[]{:S(2)}) %collective-permute-start.1) | collective-permute-done | bytes 524320 | tf_op jit(solution)/shard_map/ppermute | solution.py:463
  354.6 3.4 convolution_convert_fusion.2
  358.2 5.3 reduce-scatter.19.cloned.1.call-done
  363.5 40.5 %reduce-scatter.21.cloned.1.call-done = bf16[1,1024,384]{1,2,0:T(8,128)(2,1)} async-done(((bf16[4,1024,384]{1,2,0:T(8,128)(2,1)}), bf16[1,1024,384]{1,2,0:T(8,128)(2,1)}) %reduce-scatter.21.cloned.1.call-update) | async-done | bytes 786448 | tf_op jit(solution)/shard_map/reduce_scatter | solution.py:424
  403.9 33.6 %reduce-scatter.17.cloned.1.call-done = bf16[1,1024,256]{1,2,0:T(8,128)(2,1)} async-done(((bf16[4,1024,256]{1,2,0:T(8,128)(2,1)}), bf16[1,1024,256]{1,2,0:T(8,128)(2,1)}) %reduce-scatter.17.cloned.1.call-update) | async-done | bytes 524304 | tf_op jit(solution)/shard_map/reduce_scatter | solution.py:477
  438.2 28.8 %reduce-scatter.15.cloned.1.call-done = bf16[2,64,1024]{2,1,0:T(8,128)(2,1)} async-done(((bf16[2,256,1024]{2,1,0:T(8,128)(2,1)}), bf16[2,64,1024]{2,1,0:T(8,128)(2,1)}) %reduce-scatter.15.cloned.1.call-update) | async-done | bytes 262160 | tf_op jit(solution)/shard_map/reduce_scatter | solution.py:291
  468.2 59.8 %all-reduce.1 = bf16[2304]{0:T(1024)(128)(2,1)S(1)} all-reduce(f32[2304]{0:T(1024)S(1)} %pad_maximum_fusion.13), channel_id=12, replica_groups=mesh['rep'=2,'shard'=4,'ctx'=4] {'shard','ctx'}, use_global_device_ids=true, to_apply=%region_27.28.clone | all-reduce | flops 2304 | bytes 13824
  528.1 4.9 psum.39
  536.0 20.8 %all-reduce.5.cloned.1.call-done = (bf16[1024,256]{0,1:T(8,128)(2,1)}, bf16[1024,384]{0,1:T(8,128)(2,1)}, bf16[128,1024]{1,0:T(8,128)(2,1)}, bf16[192,1024]{1,0:T(8,128)(2,1)}) async-done(((bf16[1024,256]{0,1:T(8,128)(2,1)}, bf16[1024,384]{0,1:T(8,128)(2,1)}, bf16[128,1024]{1,0:T(8,128)(2,1)}, bf16[192,1024]{1,0:T(8,128)(2,1)}), (bf16[1024,256]{0,1:T(8,128)(2,1)}, bf16[1024,384]{0,1:T(8,128)(2,1)}, ...) | async-done | bytes 1966096 | tf_op jit(solution)/shard_map/psum | solution.py:301
  (275 shorter events, 94.3 us)
Async XLA Ops:
  7.2 53.8 %all-gather.11.cloned.1.call-start = ((), (), s32[]{:S(2)}) async-start(), calls=%async_computation.8 | async-start | bytes 1310720 | tf_op jit(solution)/shard_map/all_gather | solution.py:285
  7.9 63.8 %all-gather.23.cloned.1.call-start = ((), (), s32[]{:S(2)}) async-start(), calls=%async_computation.22 | async-start | bytes 3932160 | tf_op jit(solution)/shard_map/all_gather | solution.py:296
  10.3 9.4 %collective-permute-start = (bf16[1024,128]{1,0:T(8,128)(2,1)S(1)}, bf16[1024,128]{1,0:T(8,128)(2,1)S(1)}, u32[]{:S(2)}, u32[]{:S(2)}) collective-permute-start(bf16[1024,128]{1,0:T(8,128)(2,1)S(1)} %pad_maximum_fusion.12), channel_id=1, source_target_pairs={{0,1},{1,0},{2,3},{3,2},{4,5},{5,4},{6,7},{7,6},{8,9},{9,8},{10,11... | collective-permute-start | bytes 786440 | tf_op jit(solution)/shard_map/ppermute | solution.py:330
  20.2 40.0 %copy-start.53 = (s32[2,256]{1,0:T(2,128)S(1)}, s32[2,256]{1,0:T(2,128)}, u32[]{:S(2)}) copy-start(s32[2,256]{1,0:T(2,128)} %param.13) | copy-start | bytes 6148
  20.2 40.0 %copy-start.57 = (s32[2,256]{1,0:T(2,128)S(1)}, s32[2,256]{1,0:T(2,128)}, u32[]{:S(2)}) copy-start(s32[2,256]{1,0:T(2,128)} %param.14) | copy-start | bytes 6148
  21.5 68.4 %all-gather.13.cloned.1.call-start = ((), (), s32[]{:S(2)}) async-start(), calls=%async_computation.9 | async-start | bytes 1310720 | tf_op jit(solution)/shard_map/all_gather | solution.py:346
  22.3 98.0 %reduce-scatter.9.cloned.1.call-start = ((), (), s32[]{:S(2)}) async-start(), calls=%async_computation.10 | async-start | bytes 1310720 | tf_op jit(solution)/shard_map/reduce_scatter | solution.py:291
  92.9 56.5 %all-gather.25.cloned.1.call-start = ((), (), s32[]{:S(2)}) async-start(), calls=%async_computation.23 | async-start | bytes 3932160 | tf_op jit(solution)/shard_map/all_gather | solution.py:296
  93.9 85.4 %all-gather.15.cloned.1.call-start = ((), (), s32[]{:S(2)}) async-start(), calls=%async_computation.11 | async-start | bytes 1310720 | tf_op jit(solution)/shard_map/all_gather | solution.py:285
  123.2 85.1 %all-gather.19.cloned.1.call-start = ((), (), s32[]{:S(2)}) async-start(), calls=%async_computation.14 | async-start | bytes 1310720 | tf_op jit(solution)/shard_map/all_gather | solution.py:285
  124.0 104.9 %all-gather.17.cloned.1.call-start = ((), (), s32[]{:S(2)}) async-start(), calls=%async_computation.12 | async-start | bytes 1966080 | tf_op jit(solution)/shard_map/all_gather | solution.py:348
  124.7 150.9 %reduce-scatter.13.cloned.1.call-start = ((), (), s32[]{:S(2)}) async-start(), calls=%async_computation.15 | async-start | bytes 1310720 | tf_op jit(solution)/shard_map/reduce_scatter | solution.py:291
  248.2 31.6 %copy-start.65 = (bf16[2,256,1024]{2,1,0:T(8,128)(2,1)S(1)}, bf16[2,256,1024]{2,1,0:T(8,128)(2,1)}, u32[]{:S(2)}) copy-start(bf16[2,256,1024]{2,1,0:T(8,128)(2,1)} %all-gather.19.cloned.1.call-done) | copy-start | bytes 3145732
  248.2 58.1 %all-gather.21.cloned.1.call-start = ((), (), s32[]{:S(2)}) async-start(), calls=%async_computation.16 | async-start | bytes 1310720 | tf_op jit(solution)/shard_map/all_gather | solution.py:285
  279.7 78.5 %reduce-scatter.23.cloned.1.call-start = ((), (), s32[]{:S(2)}) async-start(), calls=%async_computation.21 | async-start | bytes 1966080 | tf_op jit(solution)/shard_map/reduce_scatter | solution.py:428
  281.9 81.6 %reduce-scatter.19.cloned.1.call-start = ((), (), s32[]{:S(2)}) async-start(), calls=%async_computation.19 | async-start | bytes 1310720 | tf_op jit(solution)/shard_map/reduce_scatter | solution.py:476
  309.3 94.7 %reduce-scatter.21.cloned.1.call-start = ((), (), s32[]{:S(2)}) async-start(), calls=%async_computation.20 | async-start | bytes 3932160 | tf_op jit(solution)/shard_map/reduce_scatter | solution.py:424
  317.7 119.8 %reduce-scatter.17.cloned.1.call-start = ((), (), s32[]{:S(2)}) async-start(), calls=%async_computation.18 | async-start | bytes 2621440 | tf_op jit(solution)/shard_map/reduce_scatter | solution.py:477
  328.9 13.8 %collective-permute-start.1 = (bf16[2,256,4,128]{1,3,2,0:T(8,128)(2,1)}, bf16[2,256,4,128]{1,3,2,0:T(8,128)(2,1)}, u32[]{:S(2)}, u32[]{:S(2)}) collective-permute-start(bf16[2,256,4,128]{1,3,2,0:T(8,128)(2,1)} %broadcast_select_fusion), channel_id=1, source_target_pairs={{0,1},{1,0},{2,3},{3,2},{4,5},{5,4},{6,7},{7,6},{8,9},{9,8},{10,11... | collective-permute-start | bytes 1572872 | tf_op jit(solution)/shard_map/ppermute | solution.py:463
  348.8 118.2 %reduce-scatter.15.cloned.1.call-start = ((), (), s32[]{:S(2)}) async-start(), calls=%async_computation.17 | async-start | bytes 1310720 | tf_op jit(solution)/shard_map/reduce_scatter | solution.py:291
  354.1 179.5 %reduce-scatter.11.cloned.1.call-start = ((), (), s32[]{:S(2)}) async-start(), calls=%async_computation.13 | async-start | bytes 1310720 | tf_op jit(solution)/shard_map/reduce_scatter | solution.py:291
  358.0 80.1 %copy-start.61 = (f32[2,64]{1,0:T(2,128)S(1)}, f32[2,64]{1,0:T(2,128)}, u32[]{:S(2)}) copy-start(f32[2,64]{1,0:T(2,128)} %get-tuple-element.68) | copy-start | bytes 1540
  358.0 109.0 %copy-start.50 = (f32[1024]{0:T(1024)S(1)}, f32[1024]{0:T(1024)}, u32[]{:S(2)}) copy-start(f32[1024]{0:T(1024)} %copy-done.49) | copy-start | bytes 12292
  358.0 110.2 %copy-start.54 = (f32[1024]{0:T(1024)S(1)}, f32[1024]{0:T(1024)}, u32[]{:S(2)}) copy-start(f32[1024]{0:T(1024)} %get-tuple-element.64) | copy-start | bytes 12292
  358.0 110.2 %copy-start.63 = (f32[128]{0:T(128)S(1)}, f32[128]{0:T(128)}, u32[]{:S(2)}) copy-start(f32[128]{0:T(128)} %get-tuple-element.62) | copy-start | bytes 1540
  358.0 175.5 %copy-start.5 = (bf16[2,64,1024]{2,1,0:T(8,128)(2,1)S(1)}, bf16[2,64,1024]{2,1,0:T(8,128)(2,1)}, u32[]{:S(2)}) copy-start(bf16[2,64,1024]{2,1,0:T(8,128)(2,1)} %reduce-scatter.9.cloned.1.call-done) | copy-start | bytes 786436
  358.0 175.5 %copy-start.15 = (bf16[2,64,1024]{2,1,0:T(8,128)(2,1)S(1)}, bf16[2,64,1024]{2,1,0:T(8,128)(2,1)}, u32[]{:S(2)}) copy-start(bf16[2,64,1024]{2,1,0:T(8,128)(2,1)} %param.15) | copy-start | bytes 786436
  358.0 175.5 %copy-start.16 = (bf16[2,64,1024]{2,1,0:T(8,128)(2,1)S(1)}, bf16[2,64,1024]{2,1,0:T(8,128)(2,1)}, u32[]{:S(2)}) copy-start(bf16[2,64,1024]{2,1,0:T(8,128)(2,1)} %reduce-scatter.13.cloned.1.call-done) | copy-start | bytes 786436
  358.0 175.5 %copy-start.48 = (f32[1024]{0:T(1024)S(1)}, f32[1024]{0:T(1024)}, u32[]{:S(2)}) copy-start(f32[1024]{0:T(1024)} %get-tuple-element.109) | copy-start | bytes 12292
  358.1 175.5 %copy-start.52 = (f32[2,64]{1,0:T(2,128)S(1)}, f32[2,64]{1,0:T(2,128)}, u32[]{:S(2)}) copy-start(f32[2,64]{1,0:T(2,128)} %copy-done.51) | copy-start | bytes 1540
  358.1 175.5 %copy-start.56 = (f32[2,64]{1,0:T(2,128)S(1)}, f32[2,64]{1,0:T(2,128)}, u32[]{:S(2)}) copy-start(f32[2,64]{1,0:T(2,128)} %copy-done.55) | copy-start | bytes 1540
  358.1 198.7 %all-reduce.5.cloned.1.call-start = ((), (), s32[]{:S(2)}) async-start(), calls=%async_computation.24 | async-start | bytes 3932160 | tf_op jit(solution)/shard_map/psum | solution.py:301
  (60 other events, 332.8 us)
Sparse Core Ops, SparseCore 0:
  9.6 31.7 all-gather.10
  43.5 28.1 all-gather.22
  73.3 16.5 all-gather.12
  93.0 27.2 reduce-scatter.8
  122.3 27.0 all-gather.24
  151.3 27.9 all-gather.14
  180.9 27.3 all-gather.18
  209.9 18.9 all-gather.16
  248.3 27.2 reduce-scatter.12
  279.8 26.4 all-gather.20
  308.8 27.3 reduce-scatter.22
  338.7 24.7 reduce-scatter.18
  366.0 37.8 reduce-scatter.20
  406.3 31.1 reduce-scatter.16
  439.6 27.2 reduce-scatter.14
  469.1 26.4 reduce-scatter.10
  498.0 58.7 all-reduce.4
